TPU v7x, 128 devices: a whole 4x4x4 slice. The times are simulated.
128 devices in a mesh: leaf: 4 (over y), rows: 32 (over z, x, core).
Axes of the slice: x: 4, y: 4, z: 4, core: 2. Of those that a mesh axis runs over, the one named last changes fastest.
Arguments:
- leaf_rhs: float32 [8, 16, 2048], P(None, 'leaf', 'rows'), may hold values from -6 to 6
- parent_rhs: float32 [8, 4, 4096], P(None, 'leaf', 'rows'), may hold values from -6 to 6
- root_rhs: float32 [8, 4096], P(None, ('leaf', 'rows')), may hold values from -6 to 6
- leaf_inv: bfloat16 [16, 2048, 2048], P('leaf', 'rows'), as said below
- leaf_panel: bfloat16 [16, 8192, 2048], P('leaf', 'rows'), may hold values from -0.0625 to 0.0625
- leaf_rows: int32 [16, 8192], P('leaf', 'rows'), may hold values from 0 to 8191, as said below
- leaf_height: int32 [16], P('leaf'), may hold values from 2048 to 8192
- parent_inv: bfloat16 [4, 4096, 4096], P('leaf', 'rows'), as said below
- parent_panel: bfloat16 [4, 4096, 4096], P('leaf', 'rows'), may hold values from -0.046875 to 0.046875
- parent_rows: int32 [4, 4096], P('leaf', 'rows'), may hold values from 0 to 4095, as said below
- parent_height: int32 [4], P('leaf'), may hold values from 1024 to 4096
- root_inv: bfloat16 [4096, 4096], P('rows'), as said below
Outputs:
- leaf_solution: float32 [8, 16, 2048], P(None, 'leaf', 'rows')
- parent_solution: float32 [8, 4, 4096], P(None, 'leaf', 'rows')
- root_solution: float32 [8, 4096], P(None, ('leaf', 'rows'))
Inputs may be any that keep to these rules, and one draw needn't show every extreme that they name: `leaf_rows`: each leaf's first leaf_height entries are distinct and ascending; every entry is a valid ancestor index. `parent_rows`: each parent's first parent_height entries are distinct and ascending. `leaf_inv`: A dense well conditioned matrix. `parent_inv`: A dense well conditioned matrix. `root_inv`: A dense well conditioned matrix.
All inputs are finite; a program needn't handle non-finite values.
Results may differ from a plain program's by a relative error of at most 0.009.
Values may be sent and summed in bfloat16 or wider, within the bound.
A program may use at most 64 MiB of HBM per device.

v0:
```python
import jax
import jax.numpy as jnp
from jax import lax
from jax.sharding import PartitionSpec as P


def shards(
    leaf_rhs,
    parent_rhs,
    root_rhs,
    leaf_inv,
    leaf_panel,
    leaf_rows,
    leaf_height,
    parent_inv,
    parent_panel,
    parent_rows,
    parent_height,
    root_inv,
):
    rcount = leaf_rhs.shape[0]
    group_leaves = leaf_rhs.shape[1]
    leaf_local = leaf_panel.shape[1]
    parent_width = parent_inv.shape[2]
    root_width = root_inv.shape[1]
    row_index = lax.axis_index("rows")
    parent_cols = parent_rhs.shape[2]
    root_cols = root_rhs.shape[1]
    flat_index = lax.axis_index("leaf") * lax.axis_size("rows") + row_index
    block = leaf_inv
    ly = jnp.einsum(
        "rln,lin->rli",
        lax.all_gather(leaf_rhs.astype(jnp.bfloat16), "rows", axis=2, tiled=True),
        block,
        preferred_element_type=jnp.float32,
    )
    lyb = ly.astype(jnp.bfloat16)
    block = leaf_panel
    lupd = jnp.einsum(
        "rln,lhn->rlh",
        lax.all_gather(lyb, "rows", axis=2, tiled=True),
        block,
        preferred_element_type=jnp.float32,
    )
    leaf_pos = row_index * leaf_local + jnp.arange(leaf_local, dtype=jnp.int32)
    leaf_mask = leaf_pos[None, :] < leaf_height[:, None]
    lupd = jnp.where(leaf_mask[None, :, :], lupd, 0.0)
    leaf_flat = leaf_rows.reshape(-1)
    local_acc = (
        jnp.zeros((rcount, parent_width + root_width), jnp.float32)
        .at[:, leaf_flat]
        .add(lupd.reshape(rcount, -1))
    )
    group_acc = lax.psum(local_acc, "rows")
    parent_acc = group_acc[:, :parent_width]
    root_from_leaves = lax.psum(group_acc[:, parent_width:], "leaf")
    parent_slice = lax.dynamic_slice_in_dim(parent_acc, row_index * parent_cols, parent_cols, 1)
    prb = (parent_rhs[:, 0, :] - parent_slice).astype(jnp.bfloat16)
    inverse_rows = parent_inv[0]
    panel_rows = parent_panel[0]
    block = inverse_rows
    py = jnp.dot(
        lax.all_gather(prb, "rows", axis=1, tiled=True), block.T, preferred_element_type=jnp.float32
    )
    pyb = py.astype(jnp.bfloat16)
    parent_local = panel_rows.shape[0]
    block = panel_rows
    pupd = jnp.dot(
        lax.all_gather(pyb, "rows", axis=1, tiled=True), block.T, preferred_element_type=jnp.float32
    )
    parent_pos = row_index * parent_local + jnp.arange(parent_local, dtype=jnp.int32)
    parent_mask = parent_pos < parent_height[0]
    pupd = jnp.where(parent_mask[None, :], pupd, 0.0)
    parent_root = jnp.zeros((rcount, root_width), jnp.float32).at[:, parent_rows[0]].add(pupd)
    root_acc = root_from_leaves + lax.psum(parent_root, ("leaf", "rows"))
    root_slice = lax.dynamic_slice_in_dim(root_acc, flat_index * root_cols, root_cols, 1)
    rrb = (root_rhs - root_slice).astype(jnp.bfloat16)
    block = root_inv
    ry = jnp.dot(
        lax.all_gather(rrb, ("leaf", "rows"), axis=1, tiled=True),
        block.T,
        preferred_element_type=jnp.float32,
    )
    root_term = jnp.dot(ry.astype(jnp.bfloat16), root_inv, preferred_element_type=jnp.float32)
    root_full = lax.psum(root_term, "rows")
    root_solution = lax.dynamic_slice_in_dim(root_full, flat_index * root_cols, root_cols, 1)
    rxb = root_full.astype(jnp.bfloat16)
    parent_anc = rxb[:, parent_rows[0]]
    parent_anc = jnp.where(parent_mask[None, :], parent_anc, jnp.zeros_like(parent_anc))
    parent_term = jnp.dot(parent_anc, panel_rows, preferred_element_type=jnp.float32)
    parent_tail = lax.psum_scatter(parent_term, "rows", scatter_dimension=1, tiled=True)
    pvb = (py - parent_tail).astype(jnp.bfloat16)
    parent_sol_term = jnp.dot(pvb, inverse_rows, preferred_element_type=jnp.float32)
    parent_sol = lax.psum_scatter(parent_sol_term, "rows", scatter_dimension=1, tiled=True)
    parent_whole = lax.all_gather(parent_sol.astype(jnp.bfloat16), "rows", axis=1, tiled=True)
    ancestors = jnp.concatenate([parent_whole, rxb], axis=1)
    leaf_anc = ancestors[:, leaf_flat].reshape(rcount, group_leaves, leaf_local)
    leaf_anc = jnp.where(leaf_mask[None, :, :], leaf_anc, jnp.zeros_like(leaf_anc))
    leaf_term = jnp.einsum("rlh,lhc->rlc", leaf_anc, leaf_panel, preferred_element_type=jnp.float32)
    leaf_tail = lax.psum_scatter(leaf_term, "rows", scatter_dimension=2, tiled=True)
    lvb = (ly - leaf_tail).astype(jnp.bfloat16)
    leaf_sol_term = jnp.einsum("rli,lic->rlc", lvb, leaf_inv, preferred_element_type=jnp.float32)
    leaf_sol = lax.psum_scatter(leaf_sol_term, "rows", scatter_dimension=2, tiled=True)
    return (leaf_sol, parent_sol[:, None, :], root_solution)


def solution(mesh):
    return jax.shard_map(
        shards,
        mesh=mesh,
        in_specs=(
            P(None, "leaf", "rows"),
            P(None, "leaf", "rows"),
            P(None, ("leaf", "rows")),
            P("leaf", "rows", None),
            P("leaf", "rows", None),
            P("leaf", "rows"),
            P("leaf"),
            P("leaf", "rows", None),
            P("leaf", "rows", None),
            P("leaf", "rows"),
            P("leaf"),
            P("rows", None),
        ),
        out_specs=(P(None, "leaf", "rows"), P(None, "leaf", "rows"), P(None, ("leaf", "rows"))),
        check_vma=False,
    )
```

profile of v0, /device:TPU:0, one launch (start us, length us, event | category | flops | bytes accessed | tf_op | source)
XLA Modules:
  0.0 916.0 jit_solution(10626270217796478974)
XLA Ops:
  8.9 27.5 %all_gather.18 = bf16[8,4,2048]{0,1,2:T(4,128)(2,1)S(1)} all-gather(bf16[8,4,64]{0,1,2:T(4,128)(2,1)S(1)} %copy.62), channel_id=1, replica_groups=mesh['leaf'=4,'rows'=32] {'rows'}, dimensions={2}, use_global_device_ids=true | all-gather | bytes 135168 | tf_op jit(solution)/shard_map/all_gather | solution.py:33
  37.3 25.3 %all_gather.19 = bf16[8,4,2048]{0,1,2:T(4,128)(2,1)S(1)} all-gather(bf16[8,4,64]{0,1,2:T(4,128)(2,1)S(1)} %copy.64), channel_id=1, replica_groups=mesh['leaf'=4,'rows'=32] {'rows'}, dimensions={2}, use_global_device_ids=true | all-gather | bytes 135168 | tf_op jit(solution)/shard_map/all_gather | solution.py:41
  62.7 3.4 fusion.6
  66.3 8.2 scatter_custom_fusion
  74.5 3.5 copy.67
  78.9 100.7 %all-reduce.5.cloned.1.call-done = f32[8,8192]{1,0:T(8,128)} async-done(((f32[8,8192]{1,0:T(8,128)}), f32[8,8192]{1,0:T(8,128)}) %all-reduce.5.cloned.1.call-update) | async-done | bytes 262160 | tf_op jit(solution)/shard_map/psum | solution.py:54
  181.2 24.6 %all_gather.20 = bf16[8,4096]{1,0:T(8,128)(2,1)S(1)} all-gather(bf16[8,128]{1,0:T(8,128)(2,1)S(1)} %subtract_convert_fusion.3), channel_id=1, replica_groups=mesh['leaf'=4,'rows'=32] {'rows'}, dimensions={1}, use_global_device_ids=true | all-gather | bytes 67584 | tf_op jit(solution)/shard_map/all_gather | solution.py:63
  206.2 21.5 %all_gather.21 = bf16[8,4096]{1,0:T(8,128)(2,1)S(1)} all-gather(bf16[8,128]{1,0:T(8,128)(2,1)S(1)} %get-tuple-element.22), channel_id=1, replica_groups=mesh['leaf'=4,'rows'=32] {'rows'}, dimensions={1}, use_global_device_ids=true | all-gather | bytes 67584 | tf_op jit(solution)/shard_map/all_gather | solution.py:69
  231.8 141.0 %all-reduce.9.cloned.1.call-done = f32[8,4096]{1,0:T(8,128)} async-done(((f32[8,4096]{1,0:T(8,128)}), f32[8,4096]{1,0:T(8,128)}) %all-reduce.9.cloned.1.call-update) | async-done | bytes 131088 | tf_op jit(solution)/shard_map/psum | solution.py:75
  372.8 41.1 %all-reduce.7.cloned.1.call-done = f32[8,4096]{1,0:T(8,128)} async-done(((f32[8,4096]{1,0:T(8,128)}), f32[8,4096]{1,0:T(8,128)}) %all-reduce.7.cloned.1.call-update) | async-done | bytes 131088 | tf_op jit(solution)/shard_map/psum | solution.py:56
  414.7 35.9 %all-gather = bf16[128,32,8]{1,2,0:T(8,128)(2,1)S(1)} all-gather(bf16[1,32,8]{1,2,0:T(8,128)(2,1)S(1)} %fusion.31), channel_id=1, replica_groups=mesh['leaf'=4,'rows'=32] {'leaf','rows'}, dimensions={0}, use_global_device_ids=true | all-gather | bytes 66048 | tf_op jit(solution)/shard_map/all_gather | solution.py:80
  450.9 3.2 fusion.13
  454.2 98.7 %all-reduce.11.cloned.1.call-done = f32[8,4096]{1,0:T(8,128)} async-done(((f32[8,4096]{1,0:T(8,128)}), f32[8,4096]{1,0:T(8,128)}) %all-reduce.11.cloned.1.call-update) | async-done | bytes 131088 | tf_op jit(solution)/shard_map/psum | solution.py:85
  558.2 71.9 %reduce-scatter.9.cloned.1.call-done = f32[8,128]{1,0:T(8,128)} async-done(((f32[8,4096]{1,0:T(8,128)}), f32[8,128]{1,0:T(8,128)}) %reduce-scatter.9.cloned.1.call-update) | async-done | bytes 4112 | tf_op jit(solution)/shard_map/reduce_scatter | solution.py:91
  631.7 73.8 %reduce-scatter.11.cloned.1.call-done = f32[8,128]{1,0:T(8,128)} async-done(((f32[8,4096]{1,0:T(8,128)}), f32[8,128]{1,0:T(8,128)}) %reduce-scatter.11.cloned.1.call-update) | async-done | bytes 4112 | tf_op jit(solution)/shard_map/reduce_scatter | solution.py:94
  706.2 23.5 %all_gather.23 = bf16[8,4096]{1,0:T(8,128)(2,1)S(1)} all-gather(bf16[8,128]{1,0:T(8,128)(2,1)S(1)} %convert_element_type.38), channel_id=1, replica_groups=mesh['leaf'=4,'rows'=32] {'rows'}, dimensions={1}, use_global_device_ids=true | all-gather | bytes 67584 | tf_op jit(solution)/shard_map/all_gather | solution.py:95
  730.7 3.2 gather_fusion.1
  734.1 2.8 convolution_bitcast_fusion.1
  736.9 3.1 copy.76
  740.0 4.5 reshape.143
  744.6 76.7 %reduce-scatter.13.cloned.1.call-done = f32[64,32]{1,0:T(8,128)} async-done(((f32[2048,32]{1,0:T(8,128)}), f32[64,32]{1,0:T(8,128)}) %reduce-scatter.13.cloned.1.call-update) | async-done | bytes 8208
  822.6 3.1 copy.78
  825.6 4.5 reshape.145
  831.6 76.0 %reduce-scatter.15.cloned.1.call-done = f32[64,32]{1,0:T(8,128)} async-done(((f32[2048,32]{1,0:T(8,128)}), f32[64,32]{1,0:T(8,128)}) %reduce-scatter.15.cloned.1.call-update) | async-done | bytes 8208
  (72 shorter events, 23.1 us)
Async XLA Ops:
  7.2 29.2 %copy-start = (bf16[4,64,2048]{2,1,0:T(8,128)(2,1)S(1)}, bf16[4,64,2048]{2,1,0:T(8,128)(2,1)}, u32[]{:S(2)}) copy-start(bf16[4,64,2048]{2,1,0:T(8,128)(2,1)} %param.15) | copy-start | bytes 3145732
  7.2 172.4 %all-reduce.5.cloned.1.call-start = ((), (), s32[]{:S(2)}) async-start(), calls=%async_computation.4 | async-start | bytes 524288 | tf_op jit(solution)/shard_map/psum | solution.py:54
  36.3 26.3 %copy-start.7 = (s32[4]{0:T(128)S(1)}, s32[4]{0:T(128)}, u32[]{:S(2)}) copy-start(s32[4]{0:T(128)} %param.18) | copy-start | bytes 52
  74.5 3.6 copy-start.8
  74.5 106.7 %copy-start.5 = (f32[8,1,128]{2,1,0:T(1,128)S(1)}, f32[8,1,128]{2,1,0:T(1,128)}, u32[]{:S(2)}) copy-start(f32[8,1,128]{2,1,0:T(1,128)} %param.13) | copy-start | bytes 12292
  74.5 131.4 %copy-start.3 = (bf16[1,128,4096]{2,1,0:T(8,128)(2,1)S(1)}, bf16[1,128,4096]{2,1,0:T(8,128)(2,1)}, u32[]{:S(2)}) copy-start(bf16[1,128,4096]{2,1,0:T(8,128)(2,1)} %param.19) | copy-start | bytes 3145732
  78.0 149.7 %copy-start.1 = (bf16[1,128,4096]{2,1,0:T(8,128)(2,1)S(1)}, bf16[1,128,4096]{2,1,0:T(8,128)(2,1)}, u32[]{:S(2)}) copy-start(bf16[1,128,4096]{2,1,0:T(8,128)(2,1)} %param.20) | copy-start | bytes 3145732
  78.1 294.8 %all-reduce.9.cloned.1.call-start = ((), (), s32[]{:S(2)}) async-start(), calls=%async_computation.6 | async-start | bytes 262144 | tf_op jit(solution)/shard_map/psum | solution.py:75
  228.2 185.7 %copy-start.6 = (f32[8,32]{1,0:T(8,128)S(1)}, f32[8,32]{1,0:T(8,128)}, u32[]{:S(2)}) copy-start(f32[8,32]{1,0:T(8,128)} %param.14) | copy-start | bytes 3076
  231.0 182.9 %all-reduce.7.cloned.1.call-start = ((), (), s32[]{:S(2)}) async-start(), calls=%async_computation.5 | async-start | bytes 262144 | tf_op jit(solution)/shard_map/psum | solution.py:56
  231.8 321.1 %all-reduce.11.cloned.1.call-start = ((), (), s32[]{:S(2)}) async-start(), calls=%async_computation.7 | async-start | bytes 262144 | tf_op jit(solution)/shard_map/psum | solution.py:85
  450.6 106.5 %copy-start.2 = (bf16[1,128,4096]{2,1,0:T(8,128)(2,1)S(1)}, bf16[1,128,4096]{2,1,0:T(8,128)(2,1)}, u32[]{:S(2)}) copy-start(bf16[1,128,4096]{2,1,0:T(8,128)(2,1)} %param.20) | copy-start | bytes 3145732
  450.9 179.2 %copy-start.4 = (bf16[1,128,4096]{2,1,0:T(8,128)(2,1)S(1)}, bf16[1,128,4096]{2,1,0:T(8,128)(2,1)}, u32[]{:S(2)}) copy-start(bf16[1,128,4096]{2,1,0:T(8,128)(2,1)} %param.19) | copy-start | bytes 3145732
  454.1 176.0 %reduce-scatter.9.cloned.1.call-start = ((), (), s32[]{:S(2)}) async-start(), calls=%async_computation.8 | async-start | bytes 135168 | tf_op jit(solution)/shard_map/reduce_scatter | solution.py:91
  558.1 147.3 %reduce-scatter.11.cloned.1.call-start = ((), (), s32[]{:S(2)}) async-start(), calls=%async_computation.9 | async-start | bytes 135168 | tf_op jit(solution)/shard_map/reduce_scatter | solution.py:94
  631.7 189.7 %reduce-scatter.13.cloned.1.call-start = ((), (), s32[]{:S(2)}) async-start(), calls=%async_computation.10 | async-start | bytes 1081344
  744.6 163.0 %reduce-scatter.15.cloned.1.call-start = ((), (), s32[]{:S(2)}) async-start(), calls=%async_computation.11 | async-start | bytes 1081344
Sparse Core Ops, SparseCore 0:
  78.2 101.3 all-reduce.4
  231.2 141.6 all-reduce.8
  375.1 38.7 all-reduce.6
  454.2 98.5 all-reduce.10
  558.3 71.7 reduce-scatter.8
  633.9 71.5 reduce-scatter.10
  744.7 76.6 reduce-scatter.12
  830.3 77.2 reduce-scatter.14
where the time goes:
time: 917 us; the launch traced here: 916 us
  waiting for transfers between devices  681 us (74%)
  blocking collectives  158 us (17%)
  local copies, waits for them, and re-layouts  35.6 us (4%)
  between operations  15 us (2%)
  matrix products  13.8 us (2%)
  other arithmetic  12.2 us (1%)
    unnamed x10, waiting for transfers between devices  154 us
    psum x1, waiting for transfers between devices, shards(): root_acc = root_from_leaves + lax.psum(parent_root, ('leaf', 'rows'))  141 us
    psum x1, waiting for transfers between devices, shards(): group_acc = lax.psum(local_acc, 'rows')  101 us
    psum x1, waiting for transfers between devices, shards(): root_full = lax.psum(root_term, 'rows')  98.7 us
    reduce_scatter x1, waiting for transfers between devices, shards(): lax.psum_scatter(parent_sol_term, 'rows', scatter_dimension=1, tiled=True)  73.8 us
    reduce_scatter x1, waiting for transfers between devices, shards(): lax.psum_scatter(parent_term, 'rows', scatter_dimension=1, tiled=True)  71.9 us
    psum x1, waiting for transfers between devices, shards(): root_from_leaves = lax.psum(group_acc[:, parent_width:], 'leaf')  41.1 us
    all_gather x1, blocking collectives, shards(): lax.all_gather(rrb, ('leaf', 'rows'), axis=1, tiled=True)  35.9 us
  transfers between devices with their start and end apart: 8, of which 8 were waited for; matrix products, arithmetic and copies ran while one was open for 0% of the time, Pallas kernels for 0%

commit v1 on v0

--- a/solution.py
+++ b/solution.py
@@ -72,7 +72,7 @@
     parent_mask = parent_pos < parent_height[0]
     pupd = jnp.where(parent_mask[None, :], pupd, 0.0)
     parent_root = jnp.zeros((rcount, root_width), jnp.float32).at[:, parent_rows[0]].add(pupd)
-    root_acc = root_from_leaves + lax.psum(parent_root, ("leaf", "rows"))
+    root_acc = root_from_leaves + jax.lax.psum(jax.lax.psum(parent_root, "rows"), "leaf")
     root_slice = lax.dynamic_slice_in_dim(root_acc, flat_index * root_cols, root_cols, 1)
     rrb = (root_rhs - root_slice).astype(jnp.bfloat16)
     block = root_inv

time: 917 us -> 877 us (0.956)
  waiting for transfers between devices: 681 us -> 640 us
    psum x1, waiting for transfers between devices: 141 us -> 101 us  [shards(): jax.lax.psum(parent_root, 'rows')]
    unnamed x29 -> x31, local copies, waits for them, and re-layouts: 19.6 us -> 19.6 us
where the time goes in v1:
time: 877 us; the launch traced here: 876 us
  waiting for transfers between devices  640 us (73%)
  blocking collectives  158 us (18%)
  local copies, waits for them, and re-layouts  35 us (4%)
  between operations  15 us (2%)
  other arithmetic  13.8 us (2%)
  matrix products  13.8 us (2%)
    unnamed x10, waiting for transfers between devices  153 us
    psum x1, waiting for transfers between devices, shards(): group_acc = lax.psum(local_acc, 'rows')  101 us
    psum x1, waiting for transfers between devices, shards(): jax.lax.psum(parent_root, 'rows')  101 us
    psum x1, waiting for transfers between devices, shards(): root_full = lax.psum(root_term, 'rows')  98.7 us
    reduce_scatter x1, waiting for transfers between devices, shards(): lax.psum_scatter(parent_sol_term, 'rows', scatter_dimension=1, tiled=True)  73.8 us
    reduce_scatter x1, waiting for transfers between devices, shards(): lax.psum_scatter(parent_term, 'rows', scatter_dimension=1, tiled=True)  71.9 us
    psum x1, waiting for transfers between devices, shards(): root_from_leaves = lax.psum(group_acc[:, parent_width:], 'leaf')  41.6 us
    all_gather x1, blocking collectives, shards(): lax.all_gather(rrb, ('leaf', 'rows'), axis=1, tiled=True)  35.9 us
  transfers between devices with their start and end apart: 8, of which 8 were waited for; matrix products, arithmetic and copies ran while one was open for 0% of the time, Pallas kernels for 0%

profile of v1, /device:TPU:0, one launch (start us, length us, event | category | flops | bytes accessed | tf_op | source)
XLA Modules:
  0.0 876.5 jit_solution(8392955872836117848)
XLA Ops:
  8.9 27.5 %all_gather.18 = bf16[8,4,2048]{0,1,2:T(4,128)(2,1)S(1)} all-gather(bf16[8,4,64]{0,1,2:T(4,128)(2,1)S(1)} %copy.62), channel_id=1, replica_groups=mesh['leaf'=4,'rows'=32] {'rows'}, dimensions={2}, use_global_device_ids=true | all-gather | bytes 135168 | tf_op jit(solution)/shard_map/all_gather | solution.py:33
  37.3 25.3 %all_gather.19 = bf16[8,4,2048]{0,1,2:T(4,128)(2,1)S(1)} all-gather(bf16[8,4,64]{0,1,2:T(4,128)(2,1)S(1)} %copy.64), channel_id=1, replica_groups=mesh['leaf'=4,'rows'=32] {'rows'}, dimensions={2}, use_global_device_ids=true | all-gather | bytes 135168 | tf_op jit(solution)/shard_map/all_gather | solution.py:41
  62.7 3.4 fusion.6
  66.3 8.2 scatter_custom_fusion
  74.5 3.6 copy.67
  78.9 100.8 %all-reduce.5.cloned.1.call-done = f32[8,8192]{1,0:T(8,128)} async-done(((f32[8,8192]{1,0:T(8,128)}), f32[8,8192]{1,0:T(8,128)}) %all-reduce.5.cloned.1.call-update) | async-done | bytes 262160 | tf_op jit(solution)/shard_map/psum | solution.py:54
  180.6 24.6 %all_gather.20 = bf16[8,4096]{1,0:T(8,128)(2,1)S(1)} all-gather(bf16[8,128]{1,0:T(8,128)(2,1)S(1)} %subtract_convert_fusion.4), channel_id=1, replica_groups=mesh['leaf'=4,'rows'=32] {'rows'}, dimensions={1}, use_global_device_ids=true | all-gather | bytes 67584 | tf_op jit(solution)/shard_map/all_gather | solution.py:63
  205.6 21.5 %all_gather.21 = bf16[8,4096]{1,0:T(8,128)(2,1)S(1)} all-gather(bf16[8,128]{1,0:T(8,128)(2,1)S(1)} %get-tuple-element.20), channel_id=1, replica_groups=mesh['leaf'=4,'rows'=32] {'rows'}, dimensions={1}, use_global_device_ids=true | all-gather | bytes 67584 | tf_op jit(solution)/shard_map/all_gather | solution.py:69
  230.5 100.7 %all-reduce.7.cloned.1.call-done = f32[8,4096]{1,0:T(8,128)} async-done(((f32[8,4096]{1,0:T(8,128)}), f32[8,4096]{1,0:T(8,128)}) %all-reduce.7.cloned.1.call-update) | async-done | bytes 131088 | tf_op jit(solution)/shard_map/psum | solution.py:75
  332.8 41.6 %all-reduce.11.cloned.1.call-done = f32[8,4096]{1,0:T(8,128)} async-done(((f32[8,4096]{1,0:T(8,128)}), f32[8,4096]{1,0:T(8,128)}) %all-reduce.11.cloned.1.call-update) | async-done | bytes 131088 | tf_op jit(solution)/shard_map/psum | solution.py:56
  375.2 35.9 %all-gather = bf16[128,32,8]{1,2,0:T(8,128)(2,1)S(1)} all-gather(bf16[1,32,8]{1,2,0:T(8,128)(2,1)S(1)} %fusion.29), channel_id=1, replica_groups=mesh['leaf'=4,'rows'=32] {'leaf','rows'}, dimensions={0}, use_global_device_ids=true | all-gather | bytes 66048 | tf_op jit(solution)/shard_map/all_gather | solution.py:80
  411.4 3.2 fusion.13
  414.6 98.7 %all-reduce.9.cloned.1.call-done = f32[8,4096]{1,0:T(8,128)} async-done(((f32[8,4096]{1,0:T(8,128)}), f32[8,4096]{1,0:T(8,128)}) %all-reduce.9.cloned.1.call-update) | async-done | bytes 131088 | tf_op jit(solution)/shard_map/psum | solution.py:85
  518.7 71.9 %reduce-scatter.9.cloned.1.call-done = f32[8,128]{1,0:T(8,128)} async-done(((f32[8,4096]{1,0:T(8,128)}), f32[8,128]{1,0:T(8,128)}) %reduce-scatter.9.cloned.1.call-update) | async-done | bytes 4112 | tf_op jit(solution)/shard_map/reduce_scatter | solution.py:91
  592.2 73.8 %reduce-scatter.11.cloned.1.call-done = f32[8,128]{1,0:T(8,128)} async-done(((f32[8,4096]{1,0:T(8,128)}), f32[8,128]{1,0:T(8,128)}) %reduce-scatter.11.cloned.1.call-update) | async-done | bytes 4112 | tf_op jit(solution)/shard_map/reduce_scatter | solution.py:94
  666.7 23.5 %all_gather.23 = bf16[8,4096]{1,0:T(8,128)(2,1)S(1)} all-gather(bf16[8,128]{1,0:T(8,128)(2,1)S(1)} %convert_element_type.38), channel_id=1, replica_groups=mesh['leaf'=4,'rows'=32] {'rows'}, dimensions={1}, use_global_device_ids=true | all-gather | bytes 67584 | tf_op jit(solution)/shard_map/all_gather | solution.py:95
  691.2 3.2 gather_fusion.1
  694.5 2.8 convolution_bitcast_fusion.1
  697.4 3.1 copy.76
  700.5 4.5 reshape.143
  705.1 76.7 %reduce-scatter.13.cloned.1.call-done = f32[64,32]{1,0:T(8,128)} async-done(((f32[2048,32]{1,0:T(8,128)}), f32[64,32]{1,0:T(8,128)}) %reduce-scatter.13.cloned.1.call-update) | async-done | bytes 8208
  783.0 3.1 copy.78
  786.1 4.5 reshape.145
  792.0 76.0 %reduce-scatter.15.cloned.1.call-done = f32[64,32]{1,0:T(8,128)} async-done(((f32[2048,32]{1,0:T(8,128)}), f32[64,32]{1,0:T(8,128)}) %reduce-scatter.15.cloned.1.call-update) | async-done | bytes 8208
  (75 shorter events, 23.3 us)
Async XLA Ops:
  7.2 29.2 %copy-start = (bf16[4,64,2048]{2,1,0:T(8,128)(2,1)S(1)}, bf16[4,64,2048]{2,1,0:T(8,128)(2,1)}, u32[]{:S(2)}) copy-start(bf16[4,64,2048]{2,1,0:T(8,128)(2,1)} %param.15) | copy-start | bytes 3145732
  7.2 172.5 %all-reduce.5.cloned.1.call-start = ((), (), s32[]{:S(2)}) async-start(), calls=%async_computation.4 | async-start | bytes 524288 | tf_op jit(solution)/shard_map/psum | solution.py:54
  36.3 26.3 %copy-start.8 = (s32[4]{0:T(128)S(1)}, s32[4]{0:T(128)}, u32[]{:S(2)}) copy-start(s32[4]{0:T(128)} %param.18) | copy-start | bytes 52
  74.5 3.7 copy-start.9
  74.5 106.1 %copy-start.6 = (f32[8,1,128]{2,1,0:T(1,128)S(1)}, f32[8,1,128]{2,1,0:T(1,128)}, u32[]{:S(2)}) copy-start(f32[8,1,128]{2,1,0:T(1,128)} %param.13) | copy-start | bytes 12292
  74.5 130.7 %copy-start.3 = (bf16[1,128,4096]{2,1,0:T(8,128)(2,1)S(1)}, bf16[1,128,4096]{2,1,0:T(8,128)(2,1)}, u32[]{:S(2)}) copy-start(bf16[1,128,4096]{2,1,0:T(8,128)(2,1)} %param.19) | copy-start | bytes 3145732
  74.5 152.6 %copy-start.1 = (bf16[1,128,4096]{2,1,0:T(8,128)(2,1)S(1)}, bf16[1,128,4096]{2,1,0:T(8,128)(2,1)}, u32[]{:S(2)}) copy-start(bf16[1,128,4096]{2,1,0:T(8,128)(2,1)} %param.20) | copy-start | bytes 3145732
  78.1 253.0 %all-reduce.7.cloned.1.call-start = ((), (), s32[]{:S(2)}) async-start(), calls=%async_computation.5 | async-start | bytes 262144 | tf_op jit(solution)/shard_map/psum | solution.py:75
  227.6 103.5 %copy-start.5 = (f32[8,8192]{1,0:T(8,128)S(1)}, f32[8,8192]{1,0:T(8,128)}, u32[]{:S(2)}) copy-start(f32[8,8192]{1,0:T(8,128)} %all-reduce.5.cloned.1.call-done) | copy-start | bytes 786436
  227.6 146.8 %copy-start.7 = (f32[8,32]{1,0:T(8,128)S(1)}, f32[8,32]{1,0:T(8,128)}, u32[]{:S(2)}) copy-start(f32[8,32]{1,0:T(8,128)} %param.14) | copy-start | bytes 3076
  230.4 144.0 %all-reduce.11.cloned.1.call-start = ((), (), s32[]{:S(2)}) async-start(), calls=%async_computation.9 | async-start | bytes 262144 | tf_op jit(solution)/shard_map/psum | solution.py:56
  332.8 180.6 %all-reduce.9.cloned.1.call-start = ((), (), s32[]{:S(2)}) async-start(), calls=%async_computation.6 | async-start | bytes 262144 | tf_op jit(solution)/shard_map/psum | solution.py:85
  411.1 106.5 %copy-start.2 = (bf16[1,128,4096]{2,1,0:T(8,128)(2,1)S(1)}, bf16[1,128,4096]{2,1,0:T(8,128)(2,1)}, u32[]{:S(2)}) copy-start(bf16[1,128,4096]{2,1,0:T(8,128)(2,1)} %param.20) | copy-start | bytes 3145732
  411.4 179.2 %copy-start.4 = (bf16[1,128,4096]{2,1,0:T(8,128)(2,1)S(1)}, bf16[1,128,4096]{2,1,0:T(8,128)(2,1)}, u32[]{:S(2)}) copy-start(bf16[1,128,4096]{2,1,0:T(8,128)(2,1)} %param.19) | copy-start | bytes 3145732
  414.6 176.0 %reduce-scatter.9.cloned.1.call-start = ((), (), s32[]{:S(2)}) async-start(), calls=%async_computation.7 | async-start | bytes 135168 | tf_op jit(solution)/shard_map/reduce_scatter | solution.py:91
  518.6 147.3 %reduce-scatter.11.cloned.1.call-start = ((), (), s32[]{:S(2)}) async-start(), calls=%async_computation.8 | async-start | bytes 135168 | tf_op jit(solution)/shard_map/reduce_scatter | solution.py:94
  592.1 189.7 %reduce-scatter.13.cloned.1.call-start = ((), (), s32[]{:S(2)}) async-start(), calls=%async_computation.10 | async-start | bytes 1081344
  705.0 163.0 %reduce-scatter.15.cloned.1.call-start = ((), (), s32[]{:S(2)}) async-start(), calls=%async_computation.11 | async-start | bytes 1081344
Sparse Core Ops, SparseCore 0:
  78.3 101.3 all-reduce.4
  230.5 100.5 all-reduce.6
  333.5 40.8 all-reduce.10
  414.7 98.5 all-reduce.8
  518.7 71.7 reduce-scatter.8
  594.4 71.5 reduce-scatter.10
  705.2 76.6 reduce-scatter.12
  790.8 77.2 reduce-scatter.14
